TPU v7x, 32 devices: a whole 2x2x4 slice. The times are simulated.
32 devices in a mesh: sky: 8 (over z, y), band: 4 (over x, core).
Axes of the slice: x: 2, y: 2, z: 4, core: 2. Of those that a mesh axis runs over, the one named last changes fastest.
Arguments:
- exposures: bfloat16 [8, 4, 1024, 1024], P('sky', 'band'), may hold values from -6 to 6
- inv_variance: bfloat16 [8, 4, 1024, 1024], P('sky', 'band'), may hold values from 0.25 to 4
- mask_planes: int32 [8, 4, 2, 35], P('sky', 'band'), may hold values from 0 to 1073741823, as said below
- sky_columns: int32 [8, 4, 8], replicated, may hold values from 0 to 7, as said below
- basis_rows: float32 [9, 25], replicated, may hold values from -1 to 1
- basis_cols: float32 [9, 25], replicated, may hold values from -1 to 1
- match_coeffs: float32 [8, 4, 9], P('sky', 'band'), may hold values from -2 to 2
- detect_taps: float32 [4, 31], P('band'), may hold values from 0.05 to 0.3
Outputs:
- difference: bfloat16 [8, 4, 1024, 1024], P('sky', 'band')
- detection: float32 [1024, 1024], P('band', 'sky')
Inputs may be any that keep to these rules, and one draw needn't show every extreme that they name: Each row sky_columns[e, b] holds 8 consecutive sky tile columns in order, counted modulo 8; every sky tile column is covered by some exposure of every band. Bit j of mask_planes[e, b, 0, w] marks pixel column 30 w + j of that exposure as bad and bit j of mask_planes[e, b, 1, w] pixel row 30 w + j; bits past 1024 are ignored. In every draw some word has all 30 bits set.
All inputs are finite; a program needn't handle non-finite values.
Results may differ from a plain program's by a relative error of at most 0.0095.
Values may be sent and summed in bfloat16 or wider, within the bound.
No kernel may reach another device: no remote copies, remote signals or barrier semaphores. Data moves between devices by JAX's collectives and lax.ppermute only.
A program may use at most 128 MiB of HBM per device.

v0:
```python
import jax
import jax.numpy as jnp
from jax import lax
from jax.sharding import PartitionSpec as P

TILE = 128
NB = 9
TAPS = 25
DTAPS = 31


def with_halo(block, sides, width):
    for axis, dim in sides:
        count = lax.axis_size(axis)
        forward = [(i, i + 1) for i in range(count - 1)]
        forward.append((count - 1, 0))
        backward = [(target, source) for source, target in forward]
        low = lax.ppermute(
            lax.slice_in_dim(block, block.shape[dim] - width, None, axis=dim), axis, forward
        )
        high = lax.ppermute(lax.slice_in_dim(block, 0, width, axis=dim), axis, backward)
        block = jnp.concatenate([low, block, high], axis=dim)
    return block


def band_matrix(tap_rows, window_width):
    offsets = (
        jnp.arange(window_width, dtype=jnp.int32)[:, None]
        - jnp.arange(TILE, dtype=jnp.int32)[None, :]
    )
    selector = (
        offsets[:, :, None] == jnp.arange(tap_rows.shape[1], dtype=jnp.int32)[None, None, :]
    ).astype(jnp.float32)
    return jnp.einsum(
        "wtl,kl->kwt", selector, tap_rows.astype(jnp.float32), precision=lax.Precision.HIGHEST
    ).astype(jnp.bfloat16)


def keep_pixels(planes, side_length):
    places = jnp.arange(side_length, dtype=jnp.int32)
    column_bits = jnp.bitwise_and(jnp.right_shift(planes[0][places // 30], places % 30), 1)
    row_bits = jnp.bitwise_and(jnp.right_shift(planes[1][places // 30], places % 30), 1)
    return jnp.logical_and(row_bits[:, None] == 0, column_bits[None, :] == 0)


def psf_match(picture, column_taps, row_taps):
    side_length = picture.shape[1]
    block_count = side_length // TILE
    margin = TAPS // 2
    width_full = TILE + 2 * margin
    padded = jnp.pad(picture, ((0, 0), (margin, margin)))
    blocks = jnp.stack(
        [
            padded[:, TILE * block_index : TILE * block_index + width_full]
            for block_index in range(block_count)
        ],
        0,
    )
    column_band = band_matrix(column_taps, width_full)
    column_pass = jnp.einsum(
        "jyw,kwt->kyjt", blocks, column_band, preferred_element_type=jnp.float32
    )
    column_pass = column_pass.reshape(NB, side_length, side_length).astype(jnp.bfloat16)
    row_padded = jnp.pad(column_pass, ((0, 0), (margin, margin), (0, 0)))
    row_blocks = jnp.stack(
        [
            row_padded[:, TILE * block_index : TILE * block_index + width_full, :]
            for block_index in range(block_count)
        ],
        0,
    )
    row_band = band_matrix(row_taps, width_full)
    summed = jnp.einsum("ikwx,kwt->itx", row_blocks, row_band, preferred_element_type=jnp.float32)
    return summed.reshape(side_length, side_length).astype(jnp.bfloat16)


def average_pieces(pieces):
    matched_in, weight_in = pieces
    weight_float = weight_in.astype(jnp.float32)
    numer = jnp.sum(weight_float * matched_in.astype(jnp.float32), axis=1)
    denom = jnp.sum(weight_float, axis=1)
    return (numer / jnp.maximum(denom, 1.0)).astype(jnp.bfloat16)


def subtract_template(template, matched, own_columns, side_length, sky_count):
    gathered = lax.all_gather(template, "sky", axis=1, tiled=True).reshape(
        side_length, sky_count, TILE
    )
    picked = jnp.take(gathered, own_columns, axis=1).reshape(side_length, side_length)
    return (matched.astype(jnp.float32) - picked.astype(jnp.float32)).astype(jnp.bfloat16)


def body(
    exposures,
    inv_variance,
    mask_planes,
    sky_columns,
    basis_rows,
    basis_cols,
    match_coeffs,
    detect_taps,
):
    picture = exposures[0, 0]
    side_length = picture.shape[0]
    block_count = side_length // TILE
    sky_count = lax.axis_size("sky")
    own_sky = lax.axis_index("sky")
    own_band = lax.axis_index("band")
    column_taps = (match_coeffs[0, 0][:, None] * basis_cols).astype(jnp.bfloat16)
    matched = psf_match(picture, column_taps, basis_rows.astype(jnp.bfloat16))
    keep = keep_pixels(mask_planes[0, 0], side_length)
    variance_inv = inv_variance[0, 0]
    weight = jnp.where(keep, variance_inv, jnp.zeros_like(variance_inv))
    own_columns = sky_columns[own_sky, own_band]
    empty_slots = jnp.zeros((side_length, sky_count, TILE), jnp.bfloat16)
    send_matched = empty_slots.at[:, own_columns, :].set(
        matched.reshape(side_length, block_count, TILE)
    )
    send_weight = empty_slots.at[:, own_columns, :].set(
        weight.reshape(side_length, block_count, TILE)
    )
    template = average_pieces(
        (
            lax.all_to_all(send_matched, "sky", split_axis=1, concat_axis=1, tiled=True),
            lax.all_to_all(send_weight, "sky", split_axis=1, concat_axis=1, tiled=True),
        )
    )
    difference = subtract_template(template, matched, own_columns, side_length, sky_count)
    margin = DTAPS // 2
    width_full = TILE + 2 * margin
    filter_band = band_matrix(detect_taps.astype(jnp.bfloat16), width_full)[0]
    widened = with_halo(template, (("sky", 1),), margin)
    smoothed = jnp.dot(widened, filter_band, preferred_element_type=jnp.float32).astype(
        jnp.bfloat16
    )
    smooth_padded = jnp.pad(smoothed, ((margin, margin), (0, 0)))
    smooth_blocks = jnp.stack(
        [
            smooth_padded[TILE * block_index : TILE * block_index + width_full]
            for block_index in range(block_count)
        ],
        0,
    )
    filtered = jnp.einsum(
        "iwx,wt->itx", smooth_blocks, filter_band, preferred_element_type=jnp.float32
    ).reshape(side_length, TILE)
    power = filtered * filtered
    detection = lax.psum_scatter(power, "band", scatter_dimension=0, tiled=True)
    return (difference[None, None], detection)


def solution(mesh):
    in_specs = (
        P("sky", "band", None, None),
        P("sky", "band", None, None),
        P("sky", "band", None, None),
        P(),
        P(),
        P(),
        P("sky", "band", None),
        P("band", None),
    )
    out_specs = (P("sky", "band", None, None), P("band", "sky"))
    return jax.shard_map(body, mesh=mesh, in_specs=in_specs, out_specs=out_specs, check_vma=False)
```

profile of v0, /device:TPU:0, one launch (start us, length us, event | category | flops | bytes accessed | tf_op | source)
XLA Modules:
  0.0 304.6 jit_solution(1016820240146248366)
XLA Ops:
  8.0 2.9 copy.65
  12.4 9.2 %convolution_convert_fusion = bf16[9,128,8,1024]{3,1,2,0:T(8,128)(2,1)} fusion(bf16[8,1024,152]{1,2,0:T(8,128)(2,1)S(1)} %fusion.34, bf16[9,152,128,1]{2,0,1,3:T(8,128)(2,1)S(1)} %fusion.19), kind=kOutput, calls=%fused_computation.5 | convolution fusion | flops 2878341120 | bytes 21714944 | tf_op jit(solution)/shard_map/jyw,kwt->kyjt/dot_general | solution.py:60
  21.6 24.6 %copy.67 = bf16[9,1024,1024]{2,1,0:T(8,128)(2,1)} copy(bf16[9,1024,1024]{1,2,0:T(8,128)(2,1)} %bitcast.237) | data formatting | bytes 37748736 | tf_op jit(solution)/shard_map/convert_element_type | solution.py:63
  46.3 4.3 %fusion.2 = bf16[8,9,152,1024]{3,2,1,0:T(8,128)(2,1)} fusion(bf16[9,1024,1024]{2,1,0:T(8,128)(2,1)} %copy.67), kind=kLoop, calls=%fused_computation.13 | loop fusion | bytes 21676032
  50.6 3.8 %copy-done = bf16[9,1024,1024]{2,1,0:T(8,128)(2,1)S(1)} copy-done((bf16[9,1024,1024]{2,1,0:T(8,128)(2,1)S(1)}, bf16[9,1024,1024]{2,1,0:T(8,128)(2,1)}, u32[]{:S(2)}) %copy-start) | copy-done | bytes 18874392
  54.4 2.5 fusion.10
  56.9 2.4 fusion.9
  59.3 2.5 fusion.8
  61.8 2.5 fusion.7
  66.7 2.4 fusion.5
  72.2 9.9 %bitcast_convert_fusion = bf16[128,8,1024]{2,0,1:T(8,128)(2,1)S(1)} fusion(bf16[8,9,152,1024]{3,2,1,0:T(8,128)(2,1)} %fusion.4, bf16[9,152,128]{2,0,1:T(8,128)(2,1)S(1)} %fusion.20), kind=kOutput, calls=%fused_computation.9 | convolution fusion | flops 2869952512 | bytes 24860672 | tf_op jit(solution)/shard_map/ikwx,kwt->itx/dot_general | solution.py:73
  86.7 5.7 %scatter_fusion.1 = bf16[1024,8,128]{2,0,1:T(8,128)(2,1)} fusion(bf16[1024,8,128]{2,0,1:T(8,128)(2,1)} %broadcast_in_dim.16.clone.1, s32[8]{0:T(128)S(1)} %fusion.61, bf16[8,1024,128]{2,1,0:T(8,128)(2,1)} %bitcast.248), kind=kCustom, calls=%fused_computation.2 | custom fusion | bytes 6291488 | tf_op jit(solution)/shard_map/scatter | solution.py:116
  92.4 7.3 %all-to-all-start.1 = ((bf16[1024,8,128]{2,0,1:T(8,128)(2,1)}), bf16[1024,8,128]{2,0,1:T(8,128)(2,1)}, u32[]{:S(2)}, u32[]{:S(2)}) async-start(bf16[1024,8,128]{2,0,1:T(8,128)(2,1)} %scatter_fusion.1), calls=%async_computation.1 | async-start | bytes 4194304 | tf_op jit(solution)/shard_map/all_to_all | solution.py:124
  99.8 3.9 %copy.75 = bf16[1,1,1024,1024]{2,3,1,0:T(8,128)(2,1)} copy(bf16[1,1,1024,1024]{3,2,1,0:T(8,128)(2,1)} %param.9) | data formatting | bytes 4194304 | tf_op args[1]
  103.7 3.9 %copy.76 = bf16[1024,8,128]{2,0,1:T(8,128)(2,1)} copy(bf16[1024,8,128]{0,2,1:T(8,128)(2,1)} %bitcast.253) | data formatting | bytes 4194304 | tf_op jit(solution)/shard_map/squeeze | solution.py:112
  110.2 4.6 %compare_select_fusion.2 = s32[1024,1]{0,1:T(1,128)S(1)} fusion(s32[]{:T(128)} %bitcast.99, s32[]{:T(128)} %bitcast.100, s32[]{:T(128)} %bitcast.101, s32[]{:T(128)} %bitcast.102, s32[]{:T(128)} %bitcast.103, s32[]{:T(128)} %bitcast.105, s32[]{:T(128)} %bitcast.104), kind=kLoop, calls=%fused_computation.125 | loop fusion | flops 23552 | bytes 4124 | tf_op jit(solution)/shard_map/gather | solution.py:41
  116.3 4.4 %compare_select_fusion.1 = s32[1024,1]{0,1:T(1,128)S(1)} fusion(s32[]{:T(128)} %bitcast.63, s32[]{:T(128)} %bitcast.64, s32[]{:T(128)} %bitcast.65, s32[]{:T(128)} %bitcast.66, s32[]{:T(128)} %bitcast.67, s32[]{:T(128)} %bitcast.69, s32[]{:T(128)} %bitcast.68), kind=kLoop, calls=%fused_computation.124 | loop fusion | flops 23552 | bytes 4124 | tf_op jit(solution)/shard_map/gather | solution.py:42
  120.6 17.6 %fusion.49 = pred[8,128]{1,0:T(8,128)(4,1)S(1)} fusion(pred[1024]{0:T(1024)(128)(4,1)S(1)} %compare_reduce_fusion, pred[1024]{0:T(1024)(128)(4,1)S(1)} %compare_reduce_fusion.1, pred[1024]{0:T(1024)(128)(4,1)S(1)} %compare_reduce_fusion.2, pred[1024]{0:T(1024)(128)(4,1)S(1)} %compare_reduce_fusion.3, pred[1024]{0:T(1024)(128)(4,1)S(1)} %compare_reduce_fusion.4, ...), kind=kLoop, calls=%fused_computation.147 | loop fusion | flops 39936 | bytes 33904 | tf_op jit(solution)/shard_map/eq | solution.py:43
  138.3 17.6 %fusion.46 = pred[1024]{0:T(1024)(128)(4,1)S(1)} fusion(pred[1024]{0:T(1024)(128)(4,1)S(1)} %compare_reduce_fusion, pred[1024]{0:T(1024)(128)(4,1)S(1)} %compare_reduce_fusion.1, pred[1024]{0:T(1024)(128)(4,1)S(1)} %compare_reduce_fusion.2, pred[1024]{0:T(1024)(128)(4,1)S(1)} %compare_reduce_fusion.3, pred[1024]{0:T(1024)(128)(4,1)S(1)} %compare_reduce_fusion.4, ...), kind=kLoop, calls=%fused_computation.144 | loop fusion | flops 37888 | bytes 33904 | tf_op jit(solution)/shard_map/eq | solution.py:43
  155.9 3.6 %fusion.16 = bf16[8,1024,128]{2,1,0:T(8,128)(2,1)} fusion(bf16[1024,8,128]{2,0,1:T(8,128)(2,1)} %copy.76, pred[8,128]{1,0:T(8,128)(4,1)S(1)} %fusion.49, pred[1024]{0:T(1024)(128)(4,1)S(1)} %fusion.46), kind=kLoop, calls=%fused_computation.35 | loop fusion | flops 2097152 | bytes 4196352 | tf_op jit(solution)/shard_map/jit(_where)/select_n | solution.py:113
  161.1 5.7 %scatter_fusion = bf16[1024,8,128]{2,0,1:T(8,128)(2,1)} fusion(bf16[1024,8,128]{2,0,1:T(8,128)(2,1)} %broadcast_in_dim.16.clone, s32[8]{0:T(128)S(1)} %fusion.61, bf16[8,1024,128]{2,1,0:T(8,128)(2,1)} %fusion.16), kind=kCustom, calls=%fused_computation.1 | custom fusion | bytes 6291488 | tf_op jit(solution)/shard_map/scatter | solution.py:119
  166.8 53.7 %all_to_all.10 = bf16[1024,8,128]{2,0,1:T(8,128)(2,1)S(1)} all-to-all(bf16[1024,8,128]{2,0,1:T(8,128)(2,1)} %scatter_fusion), channel_id=1, replica_groups=mesh['sky'=8,'band'=4] {'sky'}, dimensions={1} | all-to-all | bytes 4194304 | tf_op jit(solution)/shard_map/all_to_all | solution.py:125
  220.5 2.5 convert_reduce_fusion
  226.9 3.3 %collective-permute-start.1 = (bf16[1024,15]{1,0:T(8,128)(2,1)S(1)}, bf16[1024,15]{1,0:T(8,128)(2,1)S(1)}, u32[]{:S(2)}, u32[]{:S(2)}) collective-permute-start(bf16[1024,15]{1,0:T(8,128)(2,1)S(1)} %get-tuple-element.11), channel_id=1, source_target_pairs={{4,0},{8,4},{12,8},{16,12},{20,16},{24,20},{28,24},{0,28},{5,1},{9... | collective-permute-start | bytes 92168 | tf_op jit(solution)/shard_map/ppermute | solution.py:21
  230.7 9.0 %collective-permute-done = bf16[1024,15]{1,0:T(8,128)(2,1)S(1)} collective-permute-done((bf16[1024,15]{1,0:T(8,128)(2,1)S(1)}, bf16[1024,15]{1,0:T(8,128)(2,1)S(1)}, u32[]{:S(2)}, u32[]{:S(2)}) %collective-permute-start) | collective-permute-done | bytes 30752 | tf_op jit(solution)/shard_map/ppermute | solution.py:18
  243.6 3.2 %copy.81 = f32[1,1,1024,1024]{2,3,1,0:T(8,128)} copy(bf16[1,1,1024,1024]{3,2,1,0:T(8,128)(2,1)S(1)} %bitcast.247) | data formatting | bytes 6291456 | tf_op jit(solution)/shard_map/convert_element_type | solution.py:90
  247.6 29.6 %all-gather.2.cloned.1.call-done = bf16[1024,1024]{1,0:T(8,128)(2,1)} async-done(((bf16[1024,128]{1,0:T(8,128)(2,1)}), bf16[1024,1024]{1,0:T(8,128)(2,1)}) %all-gather.2.cloned.1.call-update) | async-done | bytes 2097168 | tf_op jit(solution)/shard_map/all_gather | solution.py:86
  277.1 3.9 %copy.78 = bf16[1024,1024]{0,1:T(8,128)(2,1)} copy(bf16[1024,1024]{1,0:T(8,128)(2,1)} %all-gather.2.cloned.1.call-done) | data formatting | bytes 4194304 | tf_op jit(solution)/shard_map/all_gather | solution.py:86
  281.1 3.0 copy.79
  286.2 2.9 copy.80
  289.1 4.1 %subtract_convert_fusion = bf16[1,1,1024,1024]{2,3,1,0:T(8,128)(2,1)} fusion(f32[1,1,1024,1024]{2,3,1,0:T(8,128)} %copy.81, bf16[1,1,1024,1024]{2,3,1,0:T(8,128)(2,1)S(1)} %bitcast.249, pred[1024]{0:T(1024)(128)(4,1)S(1)} %broadcast_bitcast_fusion), kind=kLoop, calls=%fused_computation.10 | loop fusion | flops 4194304 | bytes 8389632 | tf_op jit(solution)/shard_map/convert_element_type | solution.py:90
  293.2 3.9 %copy.82 = bf16[1,1,1024,1024]{3,2,1,0:T(8,128)(2,1)} copy(bf16[1,1,1024,1024]{2,3,1,0:T(8,128)(2,1)} %subtract_convert_fusion) | data formatting | bytes 4194304
  (90 shorter events, 28.3 us)
Async XLA Ops:
  11.1 0.7 copy-start.3
  11.1 0.7 copy-start.4
  46.3 8.2 %copy-start = (bf16[9,1024,1024]{2,1,0:T(8,128)(2,1)S(1)}, bf16[9,1024,1024]{2,1,0:T(8,128)(2,1)}, u32[]{:S(2)}) copy-start(bf16[9,1024,1024]{2,1,0:T(8,128)(2,1)} %copy.67) | copy-start | bytes 56623108
  69.2 2.4 copy-start.5
  92.4 74.4 %all-to-all-start.1 = ((bf16[1024,8,128]{2,0,1:T(8,128)(2,1)}), bf16[1024,8,128]{2,0,1:T(8,128)(2,1)}, u32[]{:S(2)}, u32[]{:S(2)}) async-start(bf16[1024,8,128]{2,0,1:T(8,128)(2,1)} %scatter_fusion.1), calls=%async_computation.1 | async-start | bytes 4194304 | tf_op jit(solution)/shard_map/all_to_all | solution.py:124
  99.8 177.4 %all-gather.2.cloned.1.call-start = ((), (), s32[]{:S(2)}) async-start(), calls=%async_computation.3 | async-start | bytes 2359296 | tf_op jit(solution)/shard_map/all_gather | solution.py:86
  103.7 5.1 %copy-start.2 = (s32[1,1,2,35]{3,2,1,0:T(2,128)S(1)}, s32[1,1,2,35]{3,2,1,0:T(2,128)}, u32[]{:S(2)}) copy-start(s32[1,1,2,35]{3,2,1,0:T(2,128)} %param.10) | copy-start | bytes 844
  222.9 7.2 %copy-start.6 = (f32[1,31]{1,0:T(1,128)S(1)}, f32[1,31]{1,0:T(1,128)}, u32[]{:S(2)}) copy-start(f32[1,31]{1,0:T(1,128)} %param.15) | copy-start | bytes 376
  223.7 18.1 %copy-start.1 = (bf16[1024,128]{1,0:T(8,128)(2,1)S(1)}, bf16[1024,128]{1,0:T(8,128)(2,1)}, u32[]{:S(2)}) copy-start(bf16[1024,128]{1,0:T(8,128)(2,1)} %divide_convert_fusion) | copy-start | bytes 786436
  223.8 73.3 %reduce-scatter.2.cloned.1.call-start = ((), (), s32[]{:S(2)}) async-start(), calls=%async_computation.4 | async-start | bytes 655360 | tf_op jit(solution)/shard_map/reduce_scatter | solution.py:148
  225.3 14.3 %collective-permute-start = (bf16[1024,15]{1,0:T(8,128)(2,1)S(1)}, bf16[1024,15]{1,0:T(8,128)(2,1)S(1)}, u32[]{:S(2)}, u32[]{:S(2)}) collective-permute-start(bf16[1024,15]{1,0:T(8,128)(2,1)S(1)} %get-tuple-element.10), channel_id=1, source_target_pairs={{0,4},{4,8},{8,12},{12,16},{16,20},{20,24},{24,28},{28,0},{1,5},{5... | collective-permute-start | bytes 92168 | tf_op jit(solution)/shard_map/ppermute | solution.py:18
  226.9 15.0 %collective-permute-start.1 = (bf16[1024,15]{1,0:T(8,128)(2,1)S(1)}, bf16[1024,15]{1,0:T(8,128)(2,1)S(1)}, u32[]{:S(2)}, u32[]{:S(2)}) collective-permute-start(bf16[1024,15]{1,0:T(8,128)(2,1)S(1)} %get-tuple-element.11), channel_id=1, source_target_pairs={{4,0},{8,4},{12,8},{16,12},{20,16},{24,20},{28,24},{0,28},{5,1},{9... | collective-permute-start | bytes 92168 | tf_op jit(solution)/shard_map/ppermute | solution.py:21
Sparse Core Ops, SparseCore 0:
  223.9 53.1 all-gather.1
Sparse Core Ops, SparseCore 1:
  243.6 20.2 reduce-scatter.1
where the time goes:
time: 307 us; the launch traced here: 305 us
  local copies, waits for them, and re-layouts  102 us (33%)
  other arithmetic  57.9 us (19%)
  blocking collectives  53.7 us (17%)
  waiting for transfers between devices  40.8 us (13%)
  matrix products  22.3 us (7%)
  between operations  15.7 us (5%)
  starting transfers between devices  12.2 us (4%)
    all_to_all x1, blocking collectives, body(): lax.all_to_all(send_weight, 'sky', split_axis=1, concat_axis=1, tiled=True)  53.7 us
    unnamed x39, local copies, waits for them, and re-layouts  35.3 us
    eq x2, other arithmetic, keep_pixels(): return jnp.logical_and(row_bits[:, None] == 0, column_bits[None, :] == 0)  35.2 us
    all_gather x1, waiting for transfers between devices, subtract_template(): lax.all_gather(template, 'sky', axis=1, tiled=True)  29.6 us
    convert_element_type x1, local copies, waits for them, and re-layouts, psf_match(): column_pass.reshape(NB, side_length, side_length).astype(jnp.bfloat16)  24.6 us
    scatter x2, local copies, waits for them, and re-layouts, body(): empty_slots.at[:, own_columns, :]  11.4 us
    dot_general x1, matrix products, psf_match(): jnp.einsum('ikwx,kwt->itx', row_blocks, row_band, preferred_element_type=...  9.89 us
    dot_general x1, matrix products, psf_match(): jnp.einsum('jyw,kwt->kyjt', blocks, column_band, preferred_element_type=j...  9.18 us
  transfers between devices with their start and end apart: 5, of which 3 were waited for; matrix products, arithmetic and copies ran while one was open for 31% of the time, Pallas kernels for 0%

commit v1 on v0

--- a/solution.py
+++ b/solution.py
@@ -7,6 +7,30 @@
 NB = 9
 TAPS = 25
 DTAPS = 31
+
+
+def cut_along(x, dim, size):
+    dims = x.shape
+    blocks = x.reshape(*dims[:dim], size, dims[dim] // size, *dims[dim + 1 :])
+    return jnp.moveaxis(blocks, dim, 0)
+
+
+def laid_out(blocks, dim):
+    lengths = list(blocks.shape[1:])
+    lengths[dim] *= blocks.shape[0]
+    return jnp.moveaxis(blocks, 0, dim).reshape(lengths)
+
+
+def sent_to_each(x, axis, split_dim, concat_dim):
+    peers, mine = (lax.axis_size(axis), lax.axis_index(axis))
+    blocks = cut_along(x, split_dim, peers)
+    out = blocks
+    for step in range(1, peers):
+        target, source = ((mine + step) % peers, (mine - step) % peers)
+        sent = lax.dynamic_index_in_dim(blocks, target, 0)
+        received = lax.ppermute(sent, axis, [(i, (i + step) % peers) for i in range(peers)])
+        out = lax.dynamic_update_slice_in_dim(out, received, source, axis=0)
+    return laid_out(out, concat_dim)
 
 
 def with_halo(block, sides, width):
@@ -122,7 +146,7 @@
     template = average_pieces(
         (
             lax.all_to_all(send_matched, "sky", split_axis=1, concat_axis=1, tiled=True),
-            lax.all_to_all(send_weight, "sky", split_axis=1, concat_axis=1, tiled=True),
+            sent_to_each(send_weight, "sky", 1, 1),
         )
     )
     difference = subtract_template(template, matched, own_columns, side_length, sky_count)

time: 307 us -> 295 us (0.961)
  blocking collectives: 53.7 us -> 0 us
  starting transfers between devices: 12.2 us -> 39.7 us
  waiting for transfers between devices: 40.8 us -> 62.6 us
  local copies, waits for them, and re-layouts: 102 us -> 96.7 us
    all_to_all x1 -> x0, blocking collectives: 53.7 us -> none  [body(): lax.all_to_all(send_weight, 'sky', split_axis=1, concat_axis=1, tiled=True)]
    ppermute x0 -> x7, waiting for transfers between devices: none -> 20.6 us  [sent_to_each(): lax.ppermute(sent, axis, [(i, (i + step) % peers) for i in range(peers)])]
    ppermute x0 -> x7, starting transfers between devices: none -> 15.7 us  [sent_to_each(): lax.ppermute(sent, axis, [(i, (i + step) % peers) for i in range(peers)])]
    ppermute x1, starting transfers between devices: 3.26 us -> 12.1 us  [with_halo(): lax.ppermute(lax.slice_in_dim(block, 0, width, axis=dim), axis, backward)]
    ppermute x1, waiting for transfers between devices: 8.96 us -> 4.07 us  [with_halo(): lax.ppermute(lax.slice_in_dim(block, block.shape[dim] - width, None, axis...]
    gather x1 -> x0, other arithmetic: 4.55 us -> none  [keep_pixels(): planes[0][places // 30]]
    gather x29 -> x15, other arithmetic: 5.49 us -> 9.26 us  [keep_pixels(): planes[1][places // 30]]
    ppermute x1, waiting for transfers between devices: 2.2 us -> 5.9 us  [with_halo(): lax.ppermute(lax.slice_in_dim(block, 0, width, axis=dim), axis, backward)]
  transfers between devices with their start and end apart: 5 -> 12, of which waited for: 3 -> 7; matrix products, arithmetic and copies ran while one was open for 31% -> 30% of each run, Pallas kernels for 0% -> 0%
where the time goes in v1:
time: 295 us; the launch traced here: 293 us
  local copies, waits for them, and re-layouts  96.7 us (33%)
  waiting for transfers between devices  62.6 us (21%)
  other arithmetic  55.6 us (19%)
  starting transfers between devices  39.7 us (13%)
  matrix products  22.3 us (8%)
  between operations  16 us (5%)
    unnamed x45, local copies, waits for them, and re-layouts  35.2 us
    eq x2, other arithmetic, keep_pixels(): return jnp.logical_and(row_bits[:, None] == 0, column_bits[None, :] == 0)  35.2 us
    all_gather x1, waiting for transfers between devices, subtract_template(): lax.all_gather(template, 'sky', axis=1, tiled=True)  32 us
    convert_element_type x1, local copies, waits for them, and re-layouts, psf_match(): column_pass.reshape(NB, side_length, side_length).astype(jnp.bfloat16)  24.6 us
    ppermute x7, waiting for transfers between devices, sent_to_each(): lax.ppermute(sent, axis, [(i, (i + step) % peers) for i in range(peers)])  20.6 us
    ppermute x7, starting transfers between devices, sent_to_each(): lax.ppermute(sent, axis, [(i, (i + step) % peers) for i in range(peers)])  15.7 us
    ppermute x1, starting transfers between devices, with_halo(): lax.ppermute(lax.slice_in_dim(block, 0, width, axis=dim), axis, backward)  12.1 us
    dot_general x1, matrix products, psf_match(): jnp.einsum('ikwx,kwt->itx', row_blocks, row_band, preferred_element_type=...  9.89 us
  transfers between devices with their start and end apart: 12, of which 7 were waited for; matrix products, arithmetic and copies ran while one was open for 30% of the time, Pallas kernels for 0%

profile of v1, /device:TPU:0, one launch (start us, length us, event | category | flops | bytes accessed | tf_op | source)
XLA Modules:
  0.0 293.0 jit_solution(2320375371692488324)
XLA Ops:
  8.0 2.9 copy.65
  12.4 9.2 %convolution_convert_fusion = bf16[9,128,8,1024]{3,1,2,0:T(8,128)(2,1)} fusion(bf16[8,1024,152]{1,2,0:T(8,128)(2,1)S(1)} %fusion.36, bf16[9,152,128,1]{2,0,1,3:T(8,128)(2,1)S(1)} %fusion.21), kind=kOutput, calls=%fused_computation.5 | convolution fusion | flops 2878341120 | bytes 21714944 | tf_op jit(solution)/shard_map/jyw,kwt->kyjt/dot_general | solution.py:84
  21.6 24.6 %copy.67 = bf16[9,1024,1024]{2,1,0:T(8,128)(2,1)} copy(bf16[9,1024,1024]{1,2,0:T(8,128)(2,1)} %bitcast.265) | data formatting | bytes 37748736 | tf_op jit(solution)/shard_map/convert_element_type | solution.py:87
  46.3 4.3 %fusion.4 = bf16[8,9,152,1024]{3,2,1,0:T(8,128)(2,1)} fusion(bf16[9,1024,1024]{2,1,0:T(8,128)(2,1)} %copy.67), kind=kLoop, calls=%fused_computation.15 | loop fusion | bytes 21676032
  50.6 3.8 %copy-done = bf16[9,1024,1024]{2,1,0:T(8,128)(2,1)S(1)} copy-done((bf16[9,1024,1024]{2,1,0:T(8,128)(2,1)S(1)}, bf16[9,1024,1024]{2,1,0:T(8,128)(2,1)}, u32[]{:S(2)}) %copy-start) | copy-done | bytes 18874392
  54.4 2.5 fusion.12
  59.3 2.5 fusion.10
  61.8 2.5 fusion.9
  72.2 9.9 %bitcast_convert_fusion = bf16[128,8,1024]{2,0,1:T(8,128)(2,1)S(1)} fusion(bf16[8,9,152,1024]{3,2,1,0:T(8,128)(2,1)} %fusion.6, bf16[9,152,128]{2,0,1:T(8,128)(2,1)S(1)} %fusion.22), kind=kOutput, calls=%fused_computation.11 | convolution fusion | flops 2869952512 | bytes 24860672 | tf_op jit(solution)/shard_map/ikwx,kwt->itx/dot_general | solution.py:97
  86.6 5.0 %scatter_fusion.1 = bf16[1024,8,128]{2,0,1:T(8,128)(2,1)} fusion(bf16[1024,8,128]{2,0,1:T(8,128)(2,1)} %broadcast_in_dim.16.clone.1, s32[8]{0:T(128)S(1)} %fusion.63, bf16[8,1024,128]{2,1,0:T(8,128)(2,1)S(1)} %bitcast.277), kind=kCustom, calls=%fused_computation.2 | custom fusion | bytes 6291488 | tf_op jit(solution)/shard_map/scatter | solution.py:140
  91.6 7.5 %all-to-all-start = ((bf16[1024,8,128]{2,0,1:T(8,128)(2,1)}), bf16[1024,8,128]{2,0,1:T(8,128)(2,1)}, u32[]{:S(2)}, u32[]{:S(2)}) async-start(bf16[1024,8,128]{2,0,1:T(8,128)(2,1)} %scatter_fusion.1), calls=%async_computation | async-start | bytes 4194304 | tf_op jit(solution)/shard_map/all_to_all | solution.py:148
  99.2 2.6 copy.75
  101.8 3.0 %copy.76 = bf16[1024,8,128]{2,0,1:T(8,128)(2,1)S(1)} copy(bf16[1024,8,128]{0,2,1:T(8,128)(2,1)} %bitcast.282) | data formatting | bytes 4194304 | tf_op jit(solution)/shard_map/squeeze | solution.py:136
  108.4 8.7 %compare_select_fusion.1 = (s32[1024,1]{0,1:T(1,128)S(1)}, s32[1024,1]{0,1:T(1,128)S(1)}) fusion(s32[]{:T(128)} %bitcast.63, s32[]{:T(128)} %bitcast.64, s32[]{:T(128)} %bitcast.65, s32[]{:T(128)} %bitcast.66, s32[]{:T(128)} %bitcast.67, s32[]{:T(128)} %bitcast.69, s32[]{:T(128)} %bitcast.68, s32[]{:T(128)} %bitcast.105, s32[]{:T(128)} %bitcast.104, ...), kind=kLoop, calls=%fused_computation.133 | loop fusion | flops 29696 | bytes 8248 | tf_op jit(solution)/shard_map/gather | solution.py:66
  117.0 17.6 %fusion.51 = pred[8,128]{1,0:T(8,128)(4,1)S(1)} fusion(pred[1024]{0:T(1024)(128)(4,1)S(1)} %get-tuple-element.87, pred[1024]{0:T(1024)(128)(4,1)S(1)} %get-tuple-element.88, pred[1024]{0:T(1024)(128)(4,1)S(1)} %get-tuple-element.89, pred[1024]{0:T(1024)(128)(4,1)S(1)} %get-tuple-element.90, pred[1024]{0:T(1024)(128)(4,1)S(1)} %get-tuple-element.91, ...), kind=kLoop, calls=%fused_computation.156 | loop fusion | flops 39936 | bytes 33904 | tf_op jit(solution)/shard_map/eq | solution.py:67
  134.6 17.6 %fusion.48 = pred[1024]{0:T(1024)(128)(4,1)S(1)} fusion(pred[1024]{0:T(1024)(128)(4,1)S(1)} %get-tuple-element.87, pred[1024]{0:T(1024)(128)(4,1)S(1)} %get-tuple-element.88, pred[1024]{0:T(1024)(128)(4,1)S(1)} %get-tuple-element.89, pred[1024]{0:T(1024)(128)(4,1)S(1)} %get-tuple-element.90, pred[1024]{0:T(1024)(128)(4,1)S(1)} %get-tuple-element.91, ...), kind=kLoop, calls=%fused_computation.153 | loop fusion | flops 37888 | bytes 33904 | tf_op jit(solution)/shard_map/eq | solution.py:67
  154.6 3.3 %scatter_fusion = bf16[1024,8,128]{2,0,1:T(8,128)(2,1)S(1)} fusion(bf16[1024,8,128]{2,0,1:T(8,128)(2,1)S(1)} %broadcast_in_dim.16.clone, s32[8]{0:T(128)S(1)} %fusion.63, bf16[8,1024,128]{2,1,0:T(8,128)(2,1)} %fusion.18), kind=kCustom, calls=%fused_computation.1 | custom fusion | bytes 6291488 | tf_op jit(solution)/shard_map/scatter | solution.py:143
  168.8 2.7 collective-permute-done
  173.3 4.4 %collective-permute-start.6 = (bf16[1,1024,1,128]{3,1,0,2:T(8,128)(2,1)}, bf16[1,1024,1,128]{3,1,0,2:T(8,128)(2,1)S(1)}, u32[]{:S(2)}, u32[]{:S(2)}) collective-permute-start(bf16[1,1024,1,128]{3,1,0,2:T(8,128)(2,1)} %get-tuple-element.8), channel_id=1, source_target_pairs={{0,28},{4,0},{8,4},{12,8},{16,12},{20,16},{24,20},{28,24},{1,29},{... | collective-permute-start | bytes 786440 | tf_op jit(solution)/shard_map/ppermute | solution.py:31
  177.7 14.8 %collective-permute-done.2 = bf16[1,1024,1,128]{3,1,0,2:T(8,128)(2,1)S(1)} collective-permute-done((bf16[1,1024,1,128]{3,1,0,2:T(8,128)(2,1)}, bf16[1,1024,1,128]{3,1,0,2:T(8,128)(2,1)S(1)}, u32[]{:S(2)}, u32[]{:S(2)}) %collective-permute-start.2) | collective-permute-done | bytes 262176 | tf_op jit(solution)/shard_map/ppermute | solution.py:31
  193.1 2.7 collective-permute-done.6
  200.7 4.4 %collective-permute-start.7 = (bf16[1024,15]{1,0:T(8,128)(2,1)S(1)}, bf16[1024,15]{1,0:T(8,128)(2,1)S(1)}, u32[]{:S(2)}, u32[]{:S(2)}) collective-permute-start(bf16[1024,15]{1,0:T(8,128)(2,1)S(1)} %get-tuple-element.15), channel_id=1, source_target_pairs={{0,4},{4,8},{8,12},{12,16},{16,20},{20,24},{24,28},{28,0},{1,5},{5... | collective-permute-start | bytes 92168 | tf_op jit(solution)/shard_map/ppermute | solution.py:42
  205.2 12.1 %collective-permute-start.8 = (bf16[1024,15]{1,0:T(8,128)(2,1)S(1)}, bf16[1024,15]{1,0:T(8,128)(2,1)S(1)}, u32[]{:S(2)}, u32[]{:S(2)}) collective-permute-start(bf16[1024,15]{1,0:T(8,128)(2,1)S(1)} %get-tuple-element.16), channel_id=1, source_target_pairs={{4,0},{8,4},{12,8},{16,12},{20,16},{24,20},{28,24},{0,28},{5,1},{9... | collective-permute-start | bytes 92168 | tf_op jit(solution)/shard_map/ppermute | solution.py:45
  217.8 4.1 %collective-permute-done.7 = bf16[1024,15]{1,0:T(8,128)(2,1)S(1)} collective-permute-done((bf16[1024,15]{1,0:T(8,128)(2,1)S(1)}, bf16[1024,15]{1,0:T(8,128)(2,1)S(1)}, u32[]{:S(2)}, u32[]{:S(2)}) %collective-permute-start.7) | collective-permute-done | bytes 30752 | tf_op jit(solution)/shard_map/ppermute | solution.py:42
  221.9 5.9 %collective-permute-done.8 = bf16[1024,15]{1,0:T(8,128)(2,1)S(1)} collective-permute-done((bf16[1024,15]{1,0:T(8,128)(2,1)S(1)}, bf16[1024,15]{1,0:T(8,128)(2,1)S(1)}, u32[]{:S(2)}, u32[]{:S(2)}) %collective-permute-start.8) | collective-permute-done | bytes 30752 | tf_op jit(solution)/shard_map/ppermute | solution.py:45
  229.5 3.2 %copy.81 = f32[1,1,1024,1024]{2,3,1,0:T(8,128)} copy(bf16[1,1,1024,1024]{3,2,1,0:T(8,128)(2,1)S(1)} %bitcast.276) | data formatting | bytes 6291456 | tf_op jit(solution)/shard_map/convert_element_type | solution.py:114
  233.5 32.0 %all-gather.2.cloned.1.call-done = bf16[1024,1024]{1,0:T(8,128)(2,1)} async-done(((bf16[1024,128]{1,0:T(8,128)(2,1)}), bf16[1024,1024]{1,0:T(8,128)(2,1)}) %all-gather.2.cloned.1.call-update) | async-done | bytes 2097168 | tf_op jit(solution)/shard_map/all_gather | solution.py:110
  265.5 3.9 %copy.78 = bf16[1024,1024]{0,1:T(8,128)(2,1)} copy(bf16[1024,1024]{1,0:T(8,128)(2,1)} %all-gather.2.cloned.1.call-done) | data formatting | bytes 4194304 | tf_op jit(solution)/shard_map/all_gather | solution.py:110
  269.5 3.0 %copy.79 = bf16[1024,8,128]{2,0,1:T(8,128)(2,1)S(1)} copy(bf16[1024,8,128]{0,2,1:T(8,128)(2,1)} %bitcast.280) | data formatting | bytes 4194304 | tf_op jit(solution)/shard_map/reshape | solution.py:110
  274.6 2.9 copy.80
  277.5 4.1 %subtract_convert_fusion = bf16[1,1,1024,1024]{2,3,1,0:T(8,128)(2,1)} fusion(f32[1,1,1024,1024]{2,3,1,0:T(8,128)} %copy.81, bf16[1,1,1024,1024]{2,3,1,0:T(8,128)(2,1)S(1)} %bitcast.278, pred[1024]{0:T(1024)(128)(4,1)S(1)} %broadcast_bitcast_fusion), kind=kLoop, calls=%fused_computation.12 | loop fusion | flops 4194304 | bytes 8389632 | tf_op jit(solution)/shard_map/convert_element_type | solution.py:114
  281.6 3.9 %copy.82 = bf16[1,1,1024,1024]{3,2,1,0:T(8,128)(2,1)} copy(bf16[1,1,1024,1024]{2,3,1,0:T(8,128)(2,1)} %subtract_convert_fusion) | data formatting | bytes 4194304
  (103 shorter events, 45.3 us)
Async XLA Ops:
  11.1 0.7 copy-start.6
  11.1 0.7 copy-start.7
  46.3 8.2 %copy-start = (bf16[9,1024,1024]{2,1,0:T(8,128)(2,1)S(1)}, bf16[9,1024,1024]{2,1,0:T(8,128)(2,1)}, u32[]{:S(2)}) copy-start(bf16[9,1024,1024]{2,1,0:T(8,128)(2,1)} %copy.67) | copy-start | bytes 56623108
  69.2 2.4 copy-start.8
  82.1 1.3 copy-start.1
  91.6 7.6 %copy-start.4 = (bf16[1,1,1024,1024]{3,2,1,0:T(8,128)(2,1)S(1)}, bf16[1,1,1024,1024]{3,2,1,0:T(8,128)(2,1)}, u32[]{:S(2)}) copy-start(bf16[1,1,1024,1024]{3,2,1,0:T(8,128)(2,1)} %param.9) | copy-start | bytes 6291460
  91.6 104.5 %all-to-all-start = ((bf16[1024,8,128]{2,0,1:T(8,128)(2,1)}), bf16[1024,8,128]{2,0,1:T(8,128)(2,1)}, u32[]{:S(2)}, u32[]{:S(2)}) async-start(bf16[1024,8,128]{2,0,1:T(8,128)(2,1)} %scatter_fusion.1), calls=%async_computation | async-start | bytes 4194304 | tf_op jit(solution)/shard_map/all_to_all | solution.py:148
  99.1 166.5 %all-gather.2.cloned.1.call-start = ((), (), s32[]{:S(2)}) async-start(), calls=%async_computation.2 | async-start | bytes 2359296 | tf_op jit(solution)/shard_map/all_gather | solution.py:110
  101.8 3.7 %copy-start.5 = (s32[1,1,2,35]{3,2,1,0:T(2,128)S(1)}, s32[1,1,2,35]{3,2,1,0:T(2,128)}, u32[]{:S(2)}) copy-start(s32[1,1,2,35]{3,2,1,0:T(2,128)} %param.10) | copy-start | bytes 844
  159.3 12.3 %collective-permute-start = (bf16[1,1024,1,128]{3,1,0,2:T(8,128)(2,1)}, bf16[1,1024,1,128]{3,1,0,2:T(8,128)(2,1)S(1)}, u32[]{:S(2)}, u32[]{:S(2)}) collective-permute-start(bf16[1,1024,1,128]{3,1,0,2:T(8,128)(2,1)} %get-tuple-element.14), channel_id=1, source_target_pairs={{0,4},{4,8},{8,12},{12,16},{16,20},{20,24},{24,28},{28,0},{1,5},{5... | collective-permute-start | bytes 786440 | tf_op jit(solution)/shard_map/ppermute | solution.py:31
  161.1 12.1 %collective-permute-start.1 = (bf16[1,1024,1,128]{3,1,0,2:T(8,128)(2,1)}, bf16[1,1024,1,128]{3,1,0,2:T(8,128)(2,1)S(1)}, u32[]{:S(2)}, u32[]{:S(2)}) collective-permute-start(bf16[1,1024,1,128]{3,1,0,2:T(8,128)(2,1)} %get-tuple-element.13), channel_id=1, source_target_pairs={{0,8},{4,12},{8,16},{12,20},{16,24},{20,28},{24,0},{28,4},{1,9},{5... | collective-permute-start | bytes 786440 | tf_op jit(solution)/shard_map/ppermute | solution.py:31
  162.6 29.9 %collective-permute-start.2 = (bf16[1,1024,1,128]{3,1,0,2:T(8,128)(2,1)}, bf16[1,1024,1,128]{3,1,0,2:T(8,128)(2,1)S(1)}, u32[]{:S(2)}, u32[]{:S(2)}) collective-permute-start(bf16[1,1024,1,128]{3,1,0,2:T(8,128)(2,1)} %get-tuple-element.12), channel_id=1, source_target_pairs={{0,12},{4,16},{8,20},{12,24},{16,28},{20,0},{24,4},{28,8},{1,13},{... | collective-permute-start | bytes 786440 | tf_op jit(solution)/shard_map/ppermute | solution.py:31
  165.0 28.0 %collective-permute-start.3 = (bf16[1,1024,1,128]{3,1,0,2:T(8,128)(2,1)}, bf16[1,1024,1,128]{3,1,0,2:T(8,128)(2,1)S(1)}, u32[]{:S(2)}, u32[]{:S(2)}) collective-permute-start(bf16[1,1024,1,128]{3,1,0,2:T(8,128)(2,1)} %get-tuple-element.11), channel_id=1, source_target_pairs={{0,16},{4,20},{8,24},{12,28},{16,0},{20,4},{24,8},{28,12},{1,17},{... | collective-permute-start | bytes 786440 | tf_op jit(solution)/shard_map/ppermute | solution.py:31
  166.4 26.6 %collective-permute-start.4 = (bf16[1,1024,1,128]{3,1,0,2:T(8,128)(2,1)}, bf16[1,1024,1,128]{3,1,0,2:T(8,128)(2,1)S(1)}, u32[]{:S(2)}, u32[]{:S(2)}) collective-permute-start(bf16[1,1024,1,128]{3,1,0,2:T(8,128)(2,1)} %get-tuple-element.10), channel_id=1, source_target_pairs={{0,20},{4,24},{8,28},{12,0},{16,4},{20,8},{24,12},{28,16},{1,21},{... | collective-permute-start | bytes 786440 | tf_op jit(solution)/shard_map/ppermute | solution.py:31
  171.5 21.5 %collective-permute-start.5 = (bf16[1,1024,1,128]{3,1,0,2:T(8,128)(2,1)}, bf16[1,1024,1,128]{3,1,0,2:T(8,128)(2,1)S(1)}, u32[]{:S(2)}, u32[]{:S(2)}) collective-permute-start(bf16[1,1024,1,128]{3,1,0,2:T(8,128)(2,1)} %get-tuple-element.9), channel_id=1, source_target_pairs={{0,24},{4,28},{8,0},{12,4},{16,8},{20,12},{24,16},{28,20},{1,25},{... | collective-permute-start | bytes 786440 | tf_op jit(solution)/shard_map/ppermute | solution.py:31
  173.3 22.5 %collective-permute-start.6 = (bf16[1,1024,1,128]{3,1,0,2:T(8,128)(2,1)}, bf16[1,1024,1,128]{3,1,0,2:T(8,128)(2,1)S(1)}, u32[]{:S(2)}, u32[]{:S(2)}) collective-permute-start(bf16[1,1024,1,128]{3,1,0,2:T(8,128)(2,1)} %get-tuple-element.8), channel_id=1, source_target_pairs={{0,28},{4,0},{8,4},{12,8},{16,12},{20,16},{24,20},{28,24},{1,29},{... | collective-permute-start | bytes 786440 | tf_op jit(solution)/shard_map/ppermute | solution.py:31
  198.3 18.9 %copy-start.9 = (f32[1,31]{1,0:T(1,128)S(1)}, f32[1,31]{1,0:T(1,128)}, u32[]{:S(2)}) copy-start(f32[1,31]{1,0:T(1,128)} %param.15) | copy-start | bytes 376
  199.1 28.6 %copy-start.3 = (bf16[1024,128]{1,0:T(8,128)(2,1)S(1)}, bf16[1024,128]{1,0:T(8,128)(2,1)}, u32[]{:S(2)}) copy-start(bf16[1024,128]{1,0:T(8,128)(2,1)} %divide_convert_fusion) | copy-start | bytes 786436
  199.2 86.4 %reduce-scatter.2.cloned.1.call-start = ((), (), s32[]{:S(2)}) async-start(), calls=%async_computation.3 | async-start | bytes 655360 | tf_op jit(solution)/shard_map/reduce_scatter | solution.py:172
  200.7 21.1 %collective-permute-start.7 = (bf16[1024,15]{1,0:T(8,128)(2,1)S(1)}, bf16[1024,15]{1,0:T(8,128)(2,1)S(1)}, u32[]{:S(2)}, u32[]{:S(2)}) collective-permute-start(bf16[1024,15]{1,0:T(8,128)(2,1)S(1)} %get-tuple-element.15), channel_id=1, source_target_pairs={{0,4},{4,8},{8,12},{12,16},{16,20},{20,24},{24,28},{28,0},{1,5},{5... | collective-permute-start | bytes 92168 | tf_op jit(solution)/shard_map/ppermute | solution.py:42
  205.2 22.6 %collective-permute-start.8 = (bf16[1024,15]{1,0:T(8,128)(2,1)S(1)}, bf16[1024,15]{1,0:T(8,128)(2,1)S(1)}, u32[]{:S(2)}, u32[]{:S(2)}) collective-permute-start(bf16[1024,15]{1,0:T(8,128)(2,1)S(1)} %get-tuple-element.16), channel_id=1, source_target_pairs={{4,0},{8,4},{12,8},{16,12},{20,16},{24,20},{28,24},{0,28},{5,1},{9... | collective-permute-start | bytes 92168 | tf_op jit(solution)/shard_map/ppermute | solution.py:45
  217.8 11.7 %copy-start.2 = (bf16[128,8,1024]{2,0,1:T(8,128)(2,1)S(1)}, bf16[128,8,1024]{2,0,1:T(8,128)(2,1)}, u32[]{:S(2)}) copy-start(bf16[128,8,1024]{2,0,1:T(8,128)(2,1)} %copy-done.1) | copy-start | bytes 6291460
Sparse Core Ops, SparseCore 0:
  199.3 66.2 all-gather.1
Sparse Core Ops, SparseCore 1:
  229.6 23.4 reduce-scatter.1
